TPU v7x, 32 devices: a whole 2x2x4 slice. The times are simulated.
32 devices in a mesh: shot: 2 (over y), depth: 2 (over core), lat: 8 (over z, x).
Axes of the slice: x: 2, y: 2, z: 4, core: 2. Of those that a mesh axis runs over, the one named last changes fastest.
Arguments:
- sources: float32 [6, 2, 32, 4096], P('shot', None, 'depth', 'lat'), parts along dimension 0, may hold values from -6 to 6
- blocks: float32 [4, 32, 7, 2, 128, 128], P(('shot', 'depth'), 'lat'), parts along dimension 0, may hold values from -0.125 to 0.125
- block_cols: int32 [2, 32, 7], P('depth', 'lat'), may hold values from 0 to 31, as said below
- refl_level: int32 [4096], P('lat'), may hold values from 0 to 1
- refl_coef: float32 [2, 4096], P(None, 'lat'), may hold values from -0.5 to 0.5
Outputs:
- bottom: float32 [6, 2, 32, 4096], P('shot', None, 'depth', 'lat'), parts along dimension 0
There are 2 independent parts, one for each index of `shot`. A program takes and returns all parts, laid end to end along the dimension named above; an argument that names none is the same for every part. Nothing has to cross between parts.
Inputs may be any that keep to these rules, and one draw needn't show every extreme that they name: block_cols[l, b, 0] = b, and every entry of row b lies within 4 block rows of b; a row may name a column twice.
All inputs are finite; a program needn't handle non-finite values.
Results may differ from a plain program's by a relative error of at most 0.0001.
Values sent between devices are 32-bit elements; how exact they have to be, the bound alone decides.
No kernel may reach another device: no remote copies, remote signals or barrier semaphores. Data moves between devices by JAX's collectives and lax.ppermute only.
A program may use at most 64 MiB of HBM per device.

v0:
```python
import jax
import jax.numpy as jnp
from jax import lax
from jax.sharding import PartitionSpec as P


def extended(value, sides, width):
    for axis, dim in sides:
        devices, length = (lax.axis_size(axis), value.shape[dim])
        up = [(i, (i + 1) % devices) for i in range(devices - 1)]
        down = [(j, i) for i, j in up]
        last = lax.slice_in_dim(value, length - width, length, axis=dim)
        initial = lax.slice_in_dim(value, 0, width, axis=dim)
        before = lax.ppermute(last, axis, up)
        after = lax.ppermute(initial, axis, down)
        value = jnp.concatenate([before, value, after], axis=dim)
    return value


def per_device(sources, blocks, block_cols, refl_level, refl_coef):
    depth_count = lax.axis_size("depth")
    lat_pos = lax.axis_index("lat")
    panels = sources.shape[0]
    src_part = sources.shape[2]
    local_points = sources.shape[3]
    level_count = blocks.shape[0]
    block_rows = blocks.shape[1]
    per_row = blocks.shape[2]
    block_size = blocks.shape[4]
    shifted_base = (lat_pos - 1) * block_rows
    every_blocks, every_cols = (
        lax.all_gather(blocks, "depth", axis=0, tiled=True),
        lax.all_gather(block_cols, "depth", axis=0, tiled=True),
    )
    wavefield = jnp.transpose(sources, (1, 0, 2, 3)).reshape(2, panels * src_part, local_points)
    for level_global in range(depth_count * level_count):
        level_blocks = every_blocks[level_global]
        level_cols = every_cols[level_global]
        channels = wavefield.shape[1]
        at_level = refl_level == level_global
        coef_re = jnp.where(at_level, refl_coef[0], jnp.float32(0.0))
        coef_im = jnp.where(at_level, refl_coef[1], jnp.float32(0.0))
        field_re = wavefield[0]
        field_im = wavefield[1]
        combined = jnp.stack(
            [
                field_re + coef_re * field_re - coef_im * field_im,
                field_im + coef_re * field_im + coef_im * field_re,
            ]
        )
        widened = extended(combined, (("lat", 2),), local_points)
        stacked = widened.reshape(2 * channels, 3 * block_rows, block_size)
        local_cols = level_cols - shifted_base
        picked = jnp.take(stacked, local_cols.reshape(-1), axis=1)
        picked = picked.reshape(2 * channels, block_rows, per_row, block_size)
        real_part = jnp.einsum(
            "cbjp,bjpq->bcq", picked, level_blocks[:, :, 0], precision=lax.Precision.HIGHEST
        )
        imag_part = jnp.einsum(
            "cbjp,bjpq->bcq", picked, level_blocks[:, :, 1], precision=lax.Precision.HIGHEST
        )
        leaving_re = real_part[:, :channels] - imag_part[:, channels:]
        leaving_im = imag_part[:, :channels] + real_part[:, channels:]
        leaving = jnp.stack([leaving_re, leaving_im])
        wavefield = jnp.transpose(leaving, (0, 2, 1, 3)).reshape(2, channels, local_points)
    result = jnp.transpose(wavefield.reshape(2, panels, src_part, local_points), (1, 0, 2, 3))
    return result


def solution(mesh):
    placed = (
        P("shot", None, "depth", "lat"),
        P(("shot", "depth"), "lat", None, None, None, None),
        P("depth", "lat", None),
        P("lat"),
        P(None, "lat"),
    )
    return jax.shard_map(
        per_device,
        mesh=mesh,
        in_specs=placed,
        out_specs=P("shot", None, "depth", "lat"),
        check_vma=False,
    )
```

profile of v0, /device:TPU:0, one launch (start us, length us, event | category | flops | bytes accessed | tf_op | source)
XLA Modules:
  0.0 67.5 jit_solution(17550229805284339037)
XLA Ops:
  6.5 0.0 copy-start.2
  6.5 0.0 copy-start.4
  6.5 0.0 copy-start.1
  6.5 0.0 copy-start.3
  6.5 0.0 all-gather.2.cloned.1.call-start
  6.6 0.7 %all-gather.2.cloned.1.call-update = ((f32[1,4,7,2,128,128]{5,4,3,2,1,0:T(8,128)}), f32[2,4,7,2,128,128]{5,4,3,2,1,0:T(8,128)}) async-update(((), (), s32[]{:S(2)}) %all-gather.2.cloned.1.call-start, f32[1,4,7,2,128,128]{5,4,3,2,1,0:T(8,128)} %param.8) | async-update | bytes 14680088
  7.3 0.0 copy-done.2
  7.3 0.0 copy-done.4
  7.3 0.2 copy-done.1
  7.6 1.3 %collective-permute-start.1 = (f32[2,48,512]{2,1,0:T(8,128)S(1)}, f32[2,48,512]{2,1,0:T(8,128)S(1)}, u32[]{:S(2)}, u32[]{:S(2)}) collective-permute-start(f32[2,48,512]{2,1,0:T(8,128)S(1)} %pad_maximum_fusion.2), channel_id=1, source_target_pairs={{1,0},{2,1},{3,2},{4,3},{5,4},{6,5},{7,6},{9,8},{10,9},{11,10},{12... | collective-permute-start | bytes 589832 | tf_op jit(solution)/shard_map/ppermute | solution.py:15
  8.9 5.5 %collective-permute-start = (f32[2,48,512]{2,1,0:T(8,128)S(1)}, f32[2,48,512]{2,1,0:T(8,128)S(1)}, u32[]{:S(2)}, u32[]{:S(2)}) collective-permute-start(f32[2,48,512]{2,1,0:T(8,128)S(1)} %pad_maximum_fusion.2), channel_id=1, source_target_pairs={{0,1},{1,2},{2,3},{3,4},{4,5},{5,6},{6,7},{8,9},{9,10},{10,11},{11... | collective-permute-start | bytes 589832 | tf_op jit(solution)/shard_map/ppermute | solution.py:14
  14.4 0.0 copy-done.3
  14.4 1.8 %all_gather.6 = s32[2,4,7]{2,1,0:T(4,128)S(1)} all-gather(s32[1,4,7]{2,1,0:T(4,128)S(1)} %copy-done.3), channel_id=1, replica_groups=mesh['shot'=2,'depth'=2,'lat'=8] {'depth'}, dimensions={0}, use_global_device_ids=true | all-gather | bytes 336 | tf_op jit(solution)/shard_map/all_gather | solution.py:33
  16.3 0.1 sub.55
  16.3 0.1 sub.51
  16.5 0.9 %collective-permute-done.1 = f32[2,48,512]{2,1,0:T(8,128)S(1)} collective-permute-done((f32[2,48,512]{2,1,0:T(8,128)S(1)}, f32[2,48,512]{2,1,0:T(8,128)S(1)}, u32[]{:S(2)}, u32[]{:S(2)}) %collective-permute-start.1) | collective-permute-done | bytes 196640 | tf_op jit(solution)/shard_map/ppermute | solution.py:15
  17.3 4.4 %collective-permute-done = f32[2,48,512]{2,1,0:T(8,128)S(1)} collective-permute-done((f32[2,48,512]{2,1,0:T(8,128)S(1)}, f32[2,48,512]{2,1,0:T(8,128)S(1)}, u32[]{:S(2)}, u32[]{:S(2)}) %collective-permute-start) | collective-permute-done | bytes 196640 | tf_op jit(solution)/shard_map/ppermute | solution.py:14
  21.8 0.1 reshape.331
  21.9 0.2 copy.24
  22.1 0.6 gather_fusion
  22.7 0.2 broadcast_select_fusion.1
  22.9 7.1 %all-gather.2.cloned.1.call-done = f32[2,4,7,2,128,128]{5,4,3,2,1,0:T(8,128)} async-done(((f32[1,4,7,2,128,128]{5,4,3,2,1,0:T(8,128)}), f32[2,4,7,2,128,128]{5,4,3,2,1,0:T(8,128)}) %all-gather.2.cloned.1.call-update) | async-done | bytes 7340048 | tf_op jit(solution)/shard_map/all_gather | solution.py:32
  29.9 4.1 %fusion.16 = (f32[1,4,7,2,128,128]{5,4,3,2,1,0:T(8,128)S(1)}, f32[1,4,7,2,128,128]{5,4,3,2,1,0:T(8,128)S(1)}) fusion(f32[2,4,7,2,128,128]{5,4,3,2,1,0:T(8,128)} %all-gather.2.cloned.1.call-done), kind=kLoop, calls=%fused_computation.54 | loop fusion | bytes 14680064 | tf_op jit(solution)/shard_map/slice | solution.py:37
  34.0 2.7 %copy_bitcast_fusion = (f32[4,7,2,128,128]{4,3,1,0,2:T(8,128)}, f32[4,7,2,128,128]{4,3,1,0,2:T(8,128)S(1)}) fusion(f32[1,4,7,2,128,128]{5,4,3,2,1,0:T(8,128)S(1)} %get-tuple-element.10, f32[1,4,7,2,128,128]{5,4,3,2,1,0:T(8,128)S(1)} %get-tuple-element.11), kind=kLoop, calls=%fused_computation.2 | loop fusion | bytes 14680064 | tf_op jit(solution)/shard_map/squeeze | solution.py:37
  36.8 1.6 %fusion.5 = f32[4,96,128]{2,1,0:T(8,128)S(1)} fusion(f32[96,4,7,128]{3,0,2,1:T(8,128)S(1)} %bitcast.66, f32[4,7,2,128,128]{4,3,1,0,2:T(8,128)S(1)} %get-tuple-element.33), kind=kOutput, calls=%fused_computation.13 | convolution fusion | flops 528482304 | bytes 3407872 | tf_op jit(solution)/shard_map/cbjp,bjpq->bcq/dot_general | solution.py:59
  38.4 1.6 %fusion.4 = f32[4,96,128]{2,1,0:T(8,128)S(1)} fusion(f32[96,4,7,128]{3,0,2,1:T(8,128)S(1)} %bitcast.67, f32[4,7,2,128,128]{4,3,1,0,2:T(8,128)S(1)} %get-tuple-element.33), kind=kOutput, calls=%fused_computation.12 | convolution fusion | flops 528482304 | bytes 3407872 | tf_op jit(solution)/shard_map/cbjp,bjpq->bcq/dot_general | solution.py:56
  40.2 1.3 %collective-permute-start.3 = (f32[2,48,512]{2,1,0:T(8,128)S(1)}, f32[2,48,512]{2,1,0:T(8,128)S(1)}, u32[]{:S(2)}, u32[]{:S(2)}) collective-permute-start(f32[2,48,512]{2,1,0:T(8,128)S(1)} %pad_maximum_fusion.3), channel_id=1, source_target_pairs={{1,0},{2,1},{3,2},{4,3},{5,4},{6,5},{7,6},{9,8},{10,9},{11,10},{12... | collective-permute-start | bytes 589832 | tf_op jit(solution)/shard_map/ppermute | solution.py:15
  41.5 4.6 %collective-permute-start.2 = (f32[2,48,512]{2,1,0:T(8,128)S(1)}, f32[2,48,512]{2,1,0:T(8,128)S(1)}, u32[]{:S(2)}, u32[]{:S(2)}) collective-permute-start(f32[2,48,512]{2,1,0:T(8,128)S(1)} %pad_maximum_fusion.3), channel_id=1, source_target_pairs={{0,1},{1,2},{2,3},{3,4},{4,5},{5,6},{6,7},{8,9},{9,10},{10,11},{11... | collective-permute-start | bytes 589832 | tf_op jit(solution)/shard_map/ppermute | solution.py:14
  46.1 3.1 %collective-permute-done.3 = f32[2,48,512]{2,1,0:T(8,128)S(1)} collective-permute-done((f32[2,48,512]{2,1,0:T(8,128)S(1)}, f32[2,48,512]{2,1,0:T(8,128)S(1)}, u32[]{:S(2)}, u32[]{:S(2)}) %collective-permute-start.3) | collective-permute-done | bytes 196640 | tf_op jit(solution)/shard_map/ppermute | solution.py:15
  49.2 4.4 %collective-permute-done.2 = f32[2,48,512]{2,1,0:T(8,128)S(1)} collective-permute-done((f32[2,48,512]{2,1,0:T(8,128)S(1)}, f32[2,48,512]{2,1,0:T(8,128)S(1)}, u32[]{:S(2)}, u32[]{:S(2)}) %collective-permute-start.2) | collective-permute-done | bytes 196640 | tf_op jit(solution)/shard_map/ppermute | solution.py:14
  53.6 0.1 reshape.333
  53.7 0.2 copy.34
  53.9 0.6 gather_fusion.1
  54.6 0.0 copy-start
  54.6 0.2 broadcast_select_fusion
  54.8 3.3 %fusion.7 = f32[4,96,128]{2,1,0:T(8,128)S(1)} fusion(f32[96,4,7,128]{3,0,2,1:T(8,128)S(1)} %bitcast.68, f32[4,7,2,128,128]{4,3,1,0,2:T(8,128)} %get-tuple-element.32), kind=kOutput, calls=%fused_computation.15 | convolution fusion | flops 528482304 | bytes 3407872 | tf_op jit(solution)/shard_map/cbjp,bjpq->bcq/dot_general | solution.py:59
  58.1 0.0 copy-done
  58.1 1.6 %fusion.6 = f32[4,96,128]{2,1,0:T(8,128)S(1)} fusion(f32[96,4,7,128]{3,0,2,1:T(8,128)S(1)} %bitcast.69, f32[4,7,2,128,128]{4,3,1,0,2:T(8,128)S(1)} %copy-done), kind=kOutput, calls=%fused_computation.14 | convolution fusion | flops 528482304 | bytes 3407872 | tf_op jit(solution)/shard_map/cbjp,bjpq->bcq/dot_general | solution.py:56
  59.8 0.1 copy.36
  59.9 0.1 reshape_reshape.3
  60.0 0.7 %copy.37 = f32[3,2,16,512]{3,2,1,0:T(8,128)} copy(f32[3,2,16,512]{3,2,0,1:T(8,128)S(1)} %bitcast.70) | data formatting | bytes 393216 | tf_op jit(solution)/shard_map/transpose | solution.py:66
  (24 shorter events, 0.4 us)
Async XLA Ops:
  6.5 0.7 %copy-start.2 = (f32[2,512]{1,0:T(2,128)S(1)}, f32[2,512]{1,0:T(2,128)}, u32[]{:S(2)}) copy-start(f32[2,512]{1,0:T(2,128)} %param.11) | copy-start | bytes 12292
  6.5 0.8 %copy-start.4 = (s32[512]{0:T(512)S(1)}, s32[512]{0:T(512)}, u32[]{:S(2)}) copy-start(s32[512]{0:T(512)} %param.10) | copy-start | bytes 6148
  6.5 1.0 %copy-start.1 = (f32[3,2,16,512]{3,2,1,0:T(8,128)S(1)}, f32[3,2,16,512]{3,2,1,0:T(8,128)}, u32[]{:S(2)}) copy-start(f32[3,2,16,512]{3,2,1,0:T(8,128)} %param.7) | copy-start | bytes 589828
  6.5 7.9 %copy-start.3 = (s32[1,4,7]{2,1,0:T(4,128)S(1)}, s32[1,4,7]{2,1,0:T(4,128)}, u32[]{:S(2)}) copy-start(s32[1,4,7]{2,1,0:T(4,128)} %param.9) | copy-start | bytes 340
  6.5 23.4 %all-gather.2.cloned.1.call-start = ((), (), s32[]{:S(2)}) async-start(), calls=%async_computation | async-start | bytes 11010048 | tf_op jit(solution)/shard_map/all_gather | solution.py:32
  7.6 9.8 %collective-permute-start.1 = (f32[2,48,512]{2,1,0:T(8,128)S(1)}, f32[2,48,512]{2,1,0:T(8,128)S(1)}, u32[]{:S(2)}, u32[]{:S(2)}) collective-permute-start(f32[2,48,512]{2,1,0:T(8,128)S(1)} %pad_maximum_fusion.2), channel_id=1, source_target_pairs={{1,0},{2,1},{3,2},{4,3},{5,4},{6,5},{7,6},{9,8},{10,9},{11,10},{12... | collective-permute-start | bytes 589832 | tf_op jit(solution)/shard_map/ppermute | solution.py:15
  8.9 12.8 %collective-permute-start = (f32[2,48,512]{2,1,0:T(8,128)S(1)}, f32[2,48,512]{2,1,0:T(8,128)S(1)}, u32[]{:S(2)}, u32[]{:S(2)}) collective-permute-start(f32[2,48,512]{2,1,0:T(8,128)S(1)} %pad_maximum_fusion.2), channel_id=1, source_target_pairs={{0,1},{1,2},{2,3},{3,4},{4,5},{5,6},{6,7},{8,9},{9,10},{10,11},{11... | collective-permute-start | bytes 589832 | tf_op jit(solution)/shard_map/ppermute | solution.py:14
  40.2 9.0 %collective-permute-start.3 = (f32[2,48,512]{2,1,0:T(8,128)S(1)}, f32[2,48,512]{2,1,0:T(8,128)S(1)}, u32[]{:S(2)}, u32[]{:S(2)}) collective-permute-start(f32[2,48,512]{2,1,0:T(8,128)S(1)} %pad_maximum_fusion.3), channel_id=1, source_target_pairs={{1,0},{2,1},{3,2},{4,3},{5,4},{6,5},{7,6},{9,8},{10,9},{11,10},{12... | collective-permute-start | bytes 589832 | tf_op jit(solution)/shard_map/ppermute | solution.py:15
  41.5 12.1 %collective-permute-start.2 = (f32[2,48,512]{2,1,0:T(8,128)S(1)}, f32[2,48,512]{2,1,0:T(8,128)S(1)}, u32[]{:S(2)}, u32[]{:S(2)}) collective-permute-start(f32[2,48,512]{2,1,0:T(8,128)S(1)} %pad_maximum_fusion.3), channel_id=1, source_target_pairs={{0,1},{1,2},{2,3},{3,4},{4,5},{5,6},{6,7},{8,9},{9,10},{10,11},{11... | collective-permute-start | bytes 589832 | tf_op jit(solution)/shard_map/ppermute | solution.py:14
  54.6 3.5 %copy-start = (f32[4,7,2,128,128]{4,3,1,0,2:T(8,128)S(1)}, f32[4,7,2,128,128]{4,3,1,0,2:T(8,128)}, u32[]{:S(2)}) copy-start(f32[4,7,2,128,128]{4,3,1,0,2:T(8,128)} %get-tuple-element.32) | copy-start | bytes 11010052
Sparse Core Ops, SparseCore 0:
  8.9 21.0 all-gather.1
where the time goes:
time: 67.7 us; the launch traced here: 67.5 us
  waiting for transfers between devices  20.5 us (30%)
  between operations  13.7 us (20%)
  starting transfers between devices  12.7 us (19%)
  local copies, waits for them, and re-layouts  10 us (15%)
  matrix products  8.14 us (12%)
  blocking collectives  1.84 us (3%)
    ppermute x2, starting transfers between devices, extended(): before = lax.ppermute(last, axis, up)  10.1 us
    ppermute x2, waiting for transfers between devices, extended(): before = lax.ppermute(last, axis, up)  8.73 us
    all_gather x1, waiting for transfers between devices, per_device(): lax.all_gather(blocks, 'depth', axis=0, tiled=True)  7.07 us
    dot_general x2, matrix products, per_device(): jnp.einsum('cbjp,bjpq->bcq', picked, level_blocks[:, :, 1], precision=lax...  4.89 us
    slice x1, local copies, waits for them, and re-layouts, per_device(): level_blocks = every_blocks[level_global]  4.09 us
    ppermute x2, waiting for transfers between devices, extended(): after = lax.ppermute(initial, axis, down)  3.98 us
    dot_general x2, matrix products, per_device(): jnp.einsum('cbjp,bjpq->bcq', picked, level_blocks[:, :, 0], precision=lax...  3.24 us
    squeeze x1, local copies, waits for them, and re-layouts, per_device(): level_blocks = every_blocks[level_global]  2.74 us
  transfers between devices with their start and end apart: 5, of which 5 were waited for; matrix products, arithmetic and copies ran while one was open for 2% of the time, Pallas kernels for 0%

commit v1 on v0

v1 whole, which is shorter than its diff:
```python
import functools

import jax
import jax.numpy as jnp
from jax import lax
from jax.experimental import pallas as pl
from jax.experimental.pallas import tpu as pltpu
from jax.sharding import PartitionSpec as P

VMEM = pl.BlockSpec(memory_space=pltpu.VMEM)
SMEM = pl.BlockSpec(memory_space=pltpu.SMEM)


def reflected(field_re, field_im, at_level, coef_re, coef_im):
    coef_re = jnp.where(at_level, coef_re, 0.0)
    coef_im = jnp.where(at_level, coef_im, 0.0)
    return (
        field_re + coef_re * field_re - coef_im * field_im,
        field_im + coef_re * field_im + coef_im * field_re,
    )


def enter_kernel(sources, refl_level, refl_coef, total):
    panels, _, part, _ = sources.shape
    at_level = refl_level[...] == 0
    for k in range(panels):
        re, im = reflected(
            sources[k, 0], sources[k, 1], at_level, refl_coef[0:1, :], refl_coef[1:2, :]
        )
        total[0, k * part : (k + 1) * part, :] = re
        total[1, k * part : (k + 1) * part, :] = im


def split_kernel(depth, own, received, high, low):
    level = pl.program_id(0)

    def write(blocks):
        for j in range(blocks.shape[2]):
            for c in range(2):
                value = blocks[0, 0, j, c]
                head = value.astype(jnp.bfloat16)
                lanes = slice(c * value.shape[1], (c + 1) * value.shape[1])
                high[0, 0, j, :, lanes] = head
                low[0, 0, j, :, lanes] = (value - head.astype(jnp.float32)).astype(
                    jnp.bfloat16
                )

    @pl.when(level == depth[0])
    def _():
        write(own)

    @pl.when(level != depth[0])
    def _():
        write(received)


def level_kernel(
    level, last, cols, where, own, swapped, diagonal, high, low, refl_level, refl_coef, out, parts
):
    _, block_rows, per_row, block_size, _ = high.shape
    channels = own.shape[1]
    rows = 2 * channels

    def place(field, first):
        for b in range(block_rows):
            lanes = slice(b * block_size, (b + 1) * block_size)
            for c in range(2):
                value = field[c, :, lanes]
                head = value.astype(jnp.bfloat16)
                at = c * channels
                parts[first + b, at : at + channels, :] = head
                parts[first + b, rows + at : rows + at + channels, :] = (
                    value - head.astype(jnp.float32)
                ).astype(jnp.bfloat16)

    place(own, block_rows)
    place(swapped, where[1])
    place(diagonal, where[2])
    for b in range(block_rows):
        picked = jnp.concatenate(
            [parts[cols[b, j] - where[0]] for j in range(per_row)], axis=1
        )
        head = high[0, b].reshape(per_row * block_size, 2 * block_size)
        tail = low[0, b].reshape(per_row * block_size, 2 * block_size)
        both = jnp.dot(picked, head, preferred_element_type=jnp.float32)
        product = (
            both[:rows]
            + both[rows:]
            + jnp.dot(picked[:rows], tail, preferred_element_type=jnp.float32)
        )
        re = product[:channels, :block_size] - product[channels:, block_size:]
        im = product[:channels, block_size:] + product[channels:, :block_size]
        lanes = slice(b * block_size, (b + 1) * block_size)
        if last:
            panels, _, part, _ = out.shape
            for k in range(panels):
                out[k, 0, :, lanes] = re[k * part : (k + 1) * part]
                out[k, 1, :, lanes] = im[k * part : (k + 1) * part]
        else:
            re, im = reflected(
                re,
                im,
                refl_level[:, lanes] == level + 1,
                refl_coef[0:1, lanes],
                refl_coef[1:2, lanes],
            )
            out[0, :, lanes] = re
            out[1, :, lanes] = im


def per_device(sources, blocks, block_cols, refl_level, refl_coef):
    lat_count = lax.axis_size("lat")
    lat_pos = lax.axis_index("lat")
    depth_pos = lax.axis_index("depth").astype(jnp.int32)
    panels, _, part, points = sources.shape
    _, block_rows, per_row, _, block_size, _ = blocks.shape
    channels = panels * part
    over_depth = [(0, 1), (1, 0)]
    pairs = [(i, i + 1) for i in range(0, lat_count - 1, 2)]
    pairs += [(j, i) for i, j in pairs]
    crossing = [(i, i + 1) for i in range(1, lat_count - 1, 2)]
    crossing += [(j, i) for i, j in crossing]
    refl_level = refl_level.reshape(1, points)

    other_blocks = lax.ppermute(blocks, "depth", over_depth)
    other_cols = lax.ppermute(block_cols, "depth", over_depth)
    total = pl.pallas_call(
        enter_kernel,
        out_shape=jax.ShapeDtypeStruct((2, channels, points), jnp.float32),
        in_specs=[VMEM] * 3,
        out_specs=VMEM,
        compiler_params=pltpu.CompilerParams(vmem_limit_bytes=4 << 20),
        name="enter",
    )(sources, refl_level, refl_coef)

    split_shape = (2, block_rows, per_row, block_size, 2 * block_size)
    block_shape = (1, 1, per_row, 2, block_size, block_size)

    def own_map(level, b, depth):
        first = jnp.where(depth[0] == 0, block_rows - 1, 0)
        return (0, jnp.where(level == depth[0], b, first), 0, 0, 0, 0)

    def received_map(level, b, depth):
        first = jnp.where(depth[0] == 1, block_rows - 1, 0)
        return (0, jnp.where(level != depth[0], b, first), 0, 0, 0, 0)

    out_block = pl.BlockSpec(
        (1, 1, per_row, block_size, 2 * block_size), lambda level, b, depth: (level, b, 0, 0, 0)
    )
    high, low = pl.pallas_call(
        split_kernel,
        out_shape=[jax.ShapeDtypeStruct(split_shape, jnp.bfloat16)] * 2,
        grid_spec=pltpu.PrefetchScalarGridSpec(
            num_scalar_prefetch=1,
            grid=(2, block_rows),
            in_specs=[
                pl.BlockSpec(block_shape, own_map),
                pl.BlockSpec(block_shape, received_map),
            ],
            out_specs=[out_block, out_block],
        ),
        cost_estimate=pl.CostEstimate(flops=0, bytes_accessed=4 * blocks.size * 4, transcendentals=0),
        compiler_params=pltpu.CompilerParams(vmem_limit_bytes=12 << 20),
        name="split",
    )(depth_pos.reshape(1), blocks, other_blocks)

    odd = (lat_pos % 2).astype(jnp.int32)
    first_row = ((lat_pos - 1) * block_rows).astype(jnp.int32)
    where = jnp.stack([first_row, 2 * block_rows * (1 - odd), 2 * block_rows * odd])
    first_cols = jnp.where(depth_pos == 0, block_cols, other_cols)[0]
    second_cols = jnp.where(depth_pos == 0, other_cols, block_cols)[0]
    for level, cols in enumerate((first_cols, second_cols)):
        last = level == 1
        diagonal = lax.ppermute(total, "lat", crossing)
        swapped = lax.ppermute(total, "lat", pairs)
        shape = (panels, 2, part, points) if last else (2, channels, points)
        level_block = pl.BlockSpec(
            (1, block_rows, per_row, block_size, 2 * block_size),
            functools.partial(lambda level, i: (level, 0, 0, 0, 0), level),
        )
        whole = pl.BlockSpec((2, channels, points), lambda i: (0, 0, 0))
        total = pl.pallas_call(
            functools.partial(level_kernel, level, last),
            out_shape=jax.ShapeDtypeStruct(shape, jnp.float32),
            grid=(1,),
            in_specs=[SMEM, SMEM, whole, whole, whole, level_block, level_block, VMEM, VMEM],
            out_specs=VMEM,
            scratch_shapes=[
                pltpu.VMEM((3 * block_rows, 4 * channels, block_size), jnp.bfloat16)
            ],
            cost_estimate=pl.CostEstimate(
                flops=12 * channels * points * per_row * block_size,
                bytes_accessed=2 * blocks.size * 4,
                transcendentals=0,
            ),
            compiler_params=pltpu.CompilerParams(vmem_limit_bytes=16 << 20),
            name="level",
        )(cols, where, total, swapped, diagonal, high, low, refl_level, refl_coef)
    return total


def solution(mesh):
    placed = (
        P("shot", None, "depth", "lat"),
        P(("shot", "depth"), "lat", None, None, None, None),
        P("depth", "lat", None),
        P("lat"),
        P(None, "lat"),
    )
    return jax.shard_map(
        per_device,
        mesh=mesh,
        in_specs=placed,
        out_specs=P("shot", None, "depth", "lat"),
        check_vma=False,
    )
```

time: 67.7 us -> 31.2 us (0.46)
  between operations: 13.7 us -> 0.08 us
  waiting for transfers between devices: 20.5 us -> 8.26 us
  Pallas kernels: 0 us -> 8.39 us
  matrix products: 8.14 us -> 0 us
  local copies, waits for them, and re-layouts: 10 us -> 4.34 us
  starting transfers between devices: 12.7 us -> 8.99 us
  blocking collectives: 1.84 us -> 0 us
    pallas_call x0 -> x4, Pallas kernels: none -> 8.39 us  [the longest x1 4.68 us: per_device(): pl.pallas_call(split_kernel, out_shape=[jax.ShapeDtypeStruct(split_shape,...]
    dot_general x4 -> x0, matrix products: 8.14 us -> none  [the longest x2 4.89 us: per_device(): jnp.einsum('cbjp,bjpq->bcq', picked, level_blocks[:, :, 1], precision=lax...]
    all_gather x1 -> x0, waiting for transfers between devices: 7.07 us -> none  [per_device(): lax.all_gather(blocks, 'depth', axis=0, tiled=True)]
    ppermute x4 -> x6, waiting for transfers between devices: 12.7 us -> 8.26 us  [the longest x2 7.18 us: per_device(): swapped = lax.ppermute(total, 'lat', pairs)]
    slice x6 -> x0, local copies, waits for them, and re-layouts: 4.21 us -> none  [the longest x1 4.09 us: per_device(): level_blocks = every_blocks[level_global]]
    unnamed x10 -> x12, local copies, waits for them, and re-layouts: 0.18 us -> 4.34 us
    ppermute x4 -> x6, starting transfers between devices: 12.7 us -> 8.99 us  [the longest x2 6.88 us: per_device(): swapped = lax.ppermute(total, 'lat', pairs)]
    squeeze x1 -> x0, local copies, waits for them, and re-layouts: 2.74 us -> none  [per_device(): level_blocks = every_blocks[level_global]]
  transfers between devices with their start and end apart: 5 -> 6, of which waited for: 5 -> 2; matrix products, arithmetic and copies ran while one was open for 2% -> 2% of each run, Pallas kernels for 0% -> 15%
where the time goes in v1:
time: 31.2 us; the launch traced here: 30.8 us
  starting transfers between devices  8.99 us (29%)
  Pallas kernels  8.39 us (27%)
  waiting for transfers between devices  8.26 us (26%)
  local copies, waits for them, and re-layouts  4.34 us (14%)
  other arithmetic  0.76 us (2%)
    ppermute x2, waiting for transfers between devices, per_device(): swapped = lax.ppermute(total, 'lat', pairs)  7.18 us
    ppermute x2, starting transfers between devices, per_device(): swapped = lax.ppermute(total, 'lat', pairs)  6.88 us
    pallas_call x1, Pallas kernels, per_device(): pl.pallas_call(split_kernel, out_shape=[jax.ShapeDtypeStruct(split_shape,...  4.68 us
    unnamed x12, local copies, waits for them, and re-layouts  4.34 us
    pallas_call x2, Pallas kernels, per_device(): pl.pallas_call(functools.partial(level_kernel, level, last), out_shape=ja...  3.68 us
    ppermute x2, starting transfers between devices, per_device(): diagonal = lax.ppermute(total, 'lat', crossing)  1.32 us
    ppermute x1, waiting for transfers between devices, per_device(): other_cols = lax.ppermute(block_cols, 'depth', over_depth)  1.07 us
    squeeze x1, other arithmetic, per_device(): first_cols = jnp.where(depth_pos == 0, block_cols, other_cols)[0]  0.68 us
  transfers between devices with their start and end apart: 6, of which 2 were waited for; matrix products, arithmetic and copies ran while one was open for 2% of the time, Pallas kernels for 15%

profile of v1, /device:TPU:0, one launch (start us, length us, event | category | flops | bytes accessed | tf_op | source)
XLA Modules:
  0.0 30.8 jit_solution(11844379146404004987)
XLA Ops:
  0.0 0.5 %collective-permute-start.3 = (f32[1,4,7,2,128,128]{5,4,3,2,1,0:T(8,128)}, f32[1,4,7,2,128,128]{5,4,3,2,1,0:T(8,128)}, u32[]{:S(2)}, u32[]{:S(2)}) collective-permute-start(f32[1,4,7,2,128,128]{5,4,3,2,1,0:T(8,128)} %own.1), channel_id=1, source_target_pairs={{0,8},{8,0},{1,9},{9,1},{2,10},{10,2},{3,11},{11,3},{4,12},{12,4},... | collective-permute-start | bytes 11010056 | tf_op jit(solution)/shard_map/ppermute | solution.py:125
  0.5 0.0 copy-start.1
  0.5 0.9 %copy-done.1 = f32[3,2,16,512]{3,2,1,0:T(8,128)S(1)} copy-done((f32[3,2,16,512]{3,2,1,0:T(8,128)S(1)}, f32[3,2,16,512]{3,2,1,0:T(8,128)}, u32[]{:S(2)}) %copy-start.1) | copy-done | bytes 196632
  1.4 0.0 copy-start.2
  1.4 0.7 %copy-done.2 = f32[2,512]{1,0:T(2,128)S(1)} copy-done((f32[2,512]{1,0:T(2,128)S(1)}, f32[2,512]{1,0:T(2,128)}, u32[]{:S(2)}) %copy-start.2) | copy-done | bytes 4120
  2.1 0.0 copy-start.4
  2.1 0.7 %copy-done.4 = s32[512]{0:T(512)S(1)} copy-done((s32[512]{0:T(512)S(1)}, s32[512]{0:T(512)}, u32[]{:S(2)}) %copy-start.4) | copy-done | bytes 2072
  2.8 2.5 %collective-permute-start.1 = (f32[2,48,512]{2,1,0:T(8,128)S(1)}, f32[2,48,512]{2,1,0:T(8,128)S(1)}, u32[]{:S(2)}, u32[]{:S(2)}) collective-permute-start(f32[2,48,512]{2,1,0:T(8,128)S(1)} %enter.1.own), channel_id=1, source_target_pairs={{0,1},{2,3},{4,5},{6,7},{1,0},{3,2},{5,4},{7,6},{8,9},{10,11},{12,... | collective-permute-start | bytes 589832 | tf_op jit(solution)/shard_map/ppermute | solution.py:175
  5.4 0.7 %collective-permute-start.2 = (f32[2,48,512]{2,1,0:T(8,128)S(1)}, f32[2,48,512]{2,1,0:T(8,128)S(1)}, u32[]{:S(2)}, u32[]{:S(2)}) collective-permute-start(f32[2,48,512]{2,1,0:T(8,128)S(1)} %enter.1.own), channel_id=1, source_target_pairs={{1,2},{3,4},{5,6},{2,1},{4,3},{6,5},{9,10},{11,12},{13,14},{10,9},... | collective-permute-start | bytes 589832 | tf_op jit(solution)/shard_map/ppermute | solution.py:174
  6.0 0.3 collective-permute-start
  6.3 0.1 pad_add_fusion.where
  6.4 1.1 %collective-permute-done = s32[1,4,7]{2,1,0:T(4,128)S(1)} collective-permute-done((s32[1,4,7]{2,1,0:T(4,128)}, s32[1,4,7]{2,1,0:T(4,128)S(1)}, u32[]{:S(2)}, u32[]{:S(2)}) %collective-permute-start) | collective-permute-done | bytes 144 | tf_op jit(solution)/shard_map/ppermute | solution.py:126
  7.5 0.7 %select_bitcast_fusion = (s32[4,7]{1,0:T(4,128)S(1)}, s32[4,7]{1,0:T(4,128)S(1)}) fusion(s32[1,4,7]{2,1,0:T(4,128)} %param.7, s32[1,4,7]{2,1,0:T(4,128)S(1)} %collective-permute-done, pred[]{:T(512)S(6)} %eq.6), kind=kLoop, calls=%fused_computation | loop fusion | flops 56 | bytes 449 | tf_op jit(solution)/shard_map/squeeze | solution.py:170
  8.2 0.0 collective-permute-done.3.received
  8.2 0.0 copy-start
  8.2 2.0 %copy-done = f32[1,4,7,2,128,128]{5,4,3,2,1,0:T(8,128)S(1)} copy-done((f32[1,4,7,2,128,128]{5,4,3,2,1,0:T(8,128)S(1)}, f32[1,4,7,2,128,128]{5,4,3,2,1,0:T(8,128)}, u32[]{:S(2)}) %copy-start) | copy-done | bytes 3670040
  10.2 0.0 copy-start.3
  10.2 0.0 copy-start.5
  10.2 4.7 %split.1 = (bf16[2,4,7,128,256]{4,3,2,1,0:T(8,128)(2,1)S(1)}, bf16[2,4,7,128,256]{4,3,2,1,0:T(8,128)(2,1)S(1)}) custom-call(s32[1]{0:T(128)} %bitcast.6.depth, f32[1,4,7,2,128,128]{5,4,3,2,1,0:T(8,128)S(1)} %copy-done, f32[1,4,7,2,128,128]{5,4,3,2,1,0:T(8,128)} %collective-permute-done.3.received), custom_call_target="tpu_custom_call" | custom-call | bytes 14680064 | tf_op jit(solution)/shard_map/split/pallas_call | solution.py:150
  14.9 0.0 collective-permute-done.1.swapped
  14.9 0.0 collective-permute-done.2.diagonal
  14.9 0.0 copy-done.3
  14.9 0.0 copy-done.5
  14.9 1.5 %level.2.own = f32[2,48,512]{2,1,0:T(8,128)S(1)} custom-call(s32[4,7]{1,0:T(4,128)S(1)} %get-tuple-element.9.cols, s32[3]{0:T(128)S(1)} %pad_add_fusion.where, f32[2,48,512]{2,1,0:T(8,128)S(1)} %enter.1.own, f32[2,48,512]{2,1,0:T(8,128)S(1)} %collective-permute-done.1.swapped, f32[2,48,512]{2,1,0:T(8,128)S(1)} %collective-permute-done.2.diagonal, ...), custom_call_target="tpu_custom_call" | custom-call | flops 264241152 | bytes 7340032 | tf_op jit(solution)/shard_map/level/pallas_call | solution.py:182
  16.4 4.3 %collective-permute-start.4 = (f32[2,48,512]{2,1,0:T(8,128)S(1)}, f32[2,48,512]{2,1,0:T(8,128)S(1)}, u32[]{:S(2)}, u32[]{:S(2)}) collective-permute-start(f32[2,48,512]{2,1,0:T(8,128)S(1)} %level.2.own), channel_id=1, source_target_pairs={{0,1},{2,3},{4,5},{6,7},{1,0},{3,2},{5,4},{7,6},{8,9},{10,11},{12,... | collective-permute-start | bytes 589832 | tf_op jit(solution)/shard_map/ppermute | solution.py:175
  20.8 0.7 %collective-permute-start.5 = (f32[2,48,512]{2,1,0:T(8,128)S(1)}, f32[2,48,512]{2,1,0:T(8,128)S(1)}, u32[]{:S(2)}, u32[]{:S(2)}) collective-permute-start(f32[2,48,512]{2,1,0:T(8,128)S(1)} %level.2.own), channel_id=1, source_target_pairs={{1,2},{3,4},{5,6},{2,1},{4,3},{6,5},{9,10},{11,12},{13,14},{10,9},... | collective-permute-start | bytes 589832 | tf_op jit(solution)/shard_map/ppermute | solution.py:174
  21.5 7.2 %collective-permute-done.4.swapped = f32[2,48,512]{2,1,0:T(8,128)S(1)} collective-permute-done((f32[2,48,512]{2,1,0:T(8,128)S(1)}, f32[2,48,512]{2,1,0:T(8,128)S(1)}, u32[]{:S(2)}, u32[]{:S(2)}) %collective-permute-start.4) | collective-permute-done | bytes 196640 | tf_op jit(solution)/shard_map/ppermute | solution.py:175
  28.6 0.0 collective-permute-done.5.diagonal
  28.6 2.2 %level.3 = f32[3,2,16,512]{3,2,1,0:T(8,128)} custom-call(s32[4,7]{1,0:T(4,128)S(1)} %get-tuple-element.10.cols, s32[3]{0:T(128)S(1)} %pad_add_fusion.where, f32[2,48,512]{2,1,0:T(8,128)S(1)} %level.2.own, f32[2,48,512]{2,1,0:T(8,128)S(1)} %collective-permute-done.4.swapped, f32[2,48,512]{2,1,0:T(8,128)S(1)} %collective-permute-done.5.diagonal, ...), custom_call_target="tpu_custom_call" | custom-call | flops 264241152 | bytes 7340032 | tf_op jit(solution)/shard_map/level/pallas_call | solution.py:182
  (1 shorter events, 0.0 us)
Async XLA Ops:
  0.0 8.2 %collective-permute-start.3 = (f32[1,4,7,2,128,128]{5,4,3,2,1,0:T(8,128)}, f32[1,4,7,2,128,128]{5,4,3,2,1,0:T(8,128)}, u32[]{:S(2)}, u32[]{:S(2)}) collective-permute-start(f32[1,4,7,2,128,128]{5,4,3,2,1,0:T(8,128)} %own.1), channel_id=1, source_target_pairs={{0,8},{8,0},{1,9},{9,1},{2,10},{10,2},{3,11},{11,3},{4,12},{12,4},... | collective-permute-start | bytes 11010056 | tf_op jit(solution)/shard_map/ppermute | solution.py:125
  0.5 0.9 %copy-start.1 = (f32[3,2,16,512]{3,2,1,0:T(8,128)S(1)}, f32[3,2,16,512]{3,2,1,0:T(8,128)}, u32[]{:S(2)}) copy-start(f32[3,2,16,512]{3,2,1,0:T(8,128)} %sources.1) | copy-start | bytes 589828
  1.4 0.7 %copy-start.2 = (f32[2,512]{1,0:T(2,128)S(1)}, f32[2,512]{1,0:T(2,128)}, u32[]{:S(2)}) copy-start(f32[2,512]{1,0:T(2,128)} %refl_coef.5) | copy-start | bytes 12292
  2.1 0.7 %copy-start.4 = (s32[512]{0:T(512)S(1)}, s32[512]{0:T(512)}, u32[]{:S(2)}) copy-start(s32[512]{0:T(512)} %param.8) | copy-start | bytes 6148
  2.8 12.1 %collective-permute-start.1 = (f32[2,48,512]{2,1,0:T(8,128)S(1)}, f32[2,48,512]{2,1,0:T(8,128)S(1)}, u32[]{:S(2)}, u32[]{:S(2)}) collective-permute-start(f32[2,48,512]{2,1,0:T(8,128)S(1)} %enter.1.own), channel_id=1, source_target_pairs={{0,1},{2,3},{4,5},{6,7},{1,0},{3,2},{5,4},{7,6},{8,9},{10,11},{12,... | collective-permute-start | bytes 589832 | tf_op jit(solution)/shard_map/ppermute | solution.py:175
  5.4 9.5 %collective-permute-start.2 = (f32[2,48,512]{2,1,0:T(8,128)S(1)}, f32[2,48,512]{2,1,0:T(8,128)S(1)}, u32[]{:S(2)}, u32[]{:S(2)}) collective-permute-start(f32[2,48,512]{2,1,0:T(8,128)S(1)} %enter.1.own), channel_id=1, source_target_pairs={{1,2},{3,4},{5,6},{2,1},{4,3},{6,5},{9,10},{11,12},{13,14},{10,9},... | collective-permute-start | bytes 589832 | tf_op jit(solution)/shard_map/ppermute | solution.py:174
  6.0 1.4 %collective-permute-start = (s32[1,4,7]{2,1,0:T(4,128)}, s32[1,4,7]{2,1,0:T(4,128)S(1)}, u32[]{:S(2)}, u32[]{:S(2)}) collective-permute-start(s32[1,4,7]{2,1,0:T(4,128)} %param.7), channel_id=1, source_target_pairs={{0,8},{8,0},{1,9},{9,1},{2,10},{10,2},{3,11},{11,3},{4,12},{12,4},... | collective-permute-start | bytes 344 | tf_op jit(solution)/shard_map/ppermute | solution.py:126
  8.2 2.0 %copy-start = (f32[1,4,7,2,128,128]{5,4,3,2,1,0:T(8,128)S(1)}, f32[1,4,7,2,128,128]{5,4,3,2,1,0:T(8,128)}, u32[]{:S(2)}) copy-start(f32[1,4,7,2,128,128]{5,4,3,2,1,0:T(8,128)} %own.1) | copy-start | bytes 11010052
  10.2 4.7 %copy-start.3 = (f32[2,512]{1,0:T(2,128)S(1)}, f32[2,512]{1,0:T(2,128)}, u32[]{:S(2)}) copy-start(f32[2,512]{1,0:T(2,128)} %refl_coef.5) | copy-start | bytes 12292
  10.2 4.7 %copy-start.5 = (s32[512]{0:T(512)S(1)}, s32[512]{0:T(512)}, u32[]{:S(2)}) copy-start(s32[512]{0:T(512)} %param.8) | copy-start | bytes 6148
  16.4 12.2 %collective-permute-start.4 = (f32[2,48,512]{2,1,0:T(8,128)S(1)}, f32[2,48,512]{2,1,0:T(8,128)S(1)}, u32[]{:S(2)}, u32[]{:S(2)}) collective-permute-start(f32[2,48,512]{2,1,0:T(8,128)S(1)} %level.2.own), channel_id=1, source_target_pairs={{0,1},{2,3},{4,5},{6,7},{1,0},{3,2},{5,4},{7,6},{8,9},{10,11},{12,... | collective-permute-start | bytes 589832 | tf_op jit(solution)/shard_map/ppermute | solution.py:175
  20.8 7.9 %collective-permute-start.5 = (f32[2,48,512]{2,1,0:T(8,128)S(1)}, f32[2,48,512]{2,1,0:T(8,128)S(1)}, u32[]{:S(2)}, u32[]{:S(2)}) collective-permute-start(f32[2,48,512]{2,1,0:T(8,128)S(1)} %level.2.own), channel_id=1, source_target_pairs={{1,2},{3,4},{5,6},{2,1},{4,3},{6,5},{9,10},{11,12},{13,14},{10,9},... | collective-permute-start | bytes 589832 | tf_op jit(solution)/shard_map/ppermute | solution.py:174

commit v2 on v0

v2 whole, which is shorter than its diff:
```python
import functools

import jax
import jax.numpy as jnp
from jax import lax
from jax.experimental import pallas as pl
from jax.experimental.pallas import tpu as pltpu
from jax.sharding import PartitionSpec as P

VMEM = pl.BlockSpec(memory_space=pltpu.VMEM)
SMEM = pl.BlockSpec(memory_space=pltpu.SMEM)
HBM = pl.BlockSpec(memory_space=pltpu.HBM)
MIB = 1 << 20


def reflected(field_re, field_im, at_level, coef_re, coef_im):
    coef_re = jnp.where(at_level, coef_re, 0.0)
    coef_im = jnp.where(at_level, coef_im, 0.0)
    return (
        field_re + coef_re * field_re - coef_im * field_im,
        field_im + coef_re * field_im + coef_im * field_re,
    )


def enter_kernel(sources, refl_level, refl_coef, total, held, level_held, coef_held, sems):
    copies = [
        pltpu.make_async_copy(a, b, sems.at[i])
        for i, (a, b) in enumerate(
            ((sources, held), (refl_level, level_held), (refl_coef, coef_held))
        )
    ]
    for copy in copies:
        copy.start()
    for copy in copies:
        copy.wait()
    panels, _, part, _ = held.shape
    at_level = level_held[...] == 0
    for k in range(panels):
        re, im = reflected(
            held[k, 0], held[k, 1], at_level, coef_held[0:1, :], coef_held[1:2, :]
        )
        total[0, k * part : (k + 1) * part, :] = re
        total[1, k * part : (k + 1) * part, :] = im


def head_and_tail(value):
    head = value.astype(jnp.bfloat16)
    return head, (value - head.astype(jnp.float32)).astype(jnp.bfloat16)


def pieces(field):
    value = field[...].reshape(field.shape[0] * field.shape[1], field.shape[2])
    return jnp.concatenate(head_and_tail(value), axis=0)


def product(left, high, low):
    rows = left.shape[0] // 2
    high = high.reshape(high.shape[0] * high.shape[1], high.shape[2])
    low = low.reshape(high.shape)
    both = jnp.dot(left, high, preferred_element_type=jnp.float32)
    cross = jnp.dot(left[:rows], low, preferred_element_type=jnp.float32)
    return both[:rows] + both[rows:] + cross


def prepare_kernel(
    level, own_cols, other_cols, own, received, field, high, low, sums, held, sems
):
    block_rows, per_row, _, size, _ = held.shape
    here = lax.axis_index("depth") == level
    first_row = lax.axis_index("lat") * block_rows
    for b in range(block_rows):

        @pl.when(here)
        def _():
            pltpu.make_async_copy(own.at[0, b], held.at[b], sems.at[b]).start()

        @pl.when(jnp.logical_not(here))
        def _():
            pltpu.make_async_copy(received.at[0, b], held.at[b], sems.at[b]).start()

    left = pieces(field)
    for b in range(block_rows):
        first = first_row + b - block_rows
        at = [
            jnp.where(here, own_cols[0, b, j], other_cols[0, b, j]) - first
            for j in range(per_row)
        ]
        for o in range(2 * block_rows + 1):
            absent = functools.reduce(jnp.logical_and, [a != o for a in at])

            @pl.when(absent)
            def _():
                zeros = jnp.zeros((size, 2 * size), jnp.bfloat16)
                high[b, o] = zeros
                low[b, o] = zeros

        same = [[at[i] == at[j] for i in range(j)] for j in range(per_row)]
        repeated = functools.reduce(jnp.logical_or, sum(same, []))
        pltpu.make_async_copy(own.at[0, b], held.at[b], sems.at[b]).wait()

        @pl.when(repeated)
        def _():
            for j in reversed(range(1, per_row)):
                unmerged = True
                for i in reversed(range(j)):

                    @pl.when(jnp.logical_and(same[j][i], unmerged))
                    def _():
                        held[b, i] = held[b, i] + held[b, j]

                    unmerged = jnp.logical_and(unmerged, jnp.logical_not(same[j][i]))

        for j in reversed(range(per_row)):
            for c in range(2):
                head, tail = head_and_tail(held[b, j, c])
                high[b, at[j], :, c * size : (c + 1) * size] = head
                low[b, at[j], :, c * size : (c + 1) * size] = tail
        band = slice(block_rows - b, 2 * block_rows - b)
        sums[b] = product(left, high[b, band], low[b, band])


def add_halo(halo, high, low, is_left, add):
    block_rows, span, size, _ = high.shape
    left = pieces(halo)

    @pl.when(is_left)
    def _():
        for b in range(block_rows):
            band = slice(0, block_rows - b)
            add(b, product(left[:, b * size :], high[b, band], low[b, band]))

    @pl.when(jnp.logical_not(is_left))
    def _():
        for b in range(block_rows):
            band = slice(span - 1 - b, span)
            add(b, product(left[:, : (b + 1) * size], high[b, band], low[b, band]))


def first_halo_kernel(halo, high, low, sums, out):
    def add(b, value):
        out[b] = sums[b] + value

    add_halo(halo, high, low, lax.axis_index("lat") % 2 == 1, add)


def leaving(value):
    channels, size = value.shape[0] // 2, value.shape[1] // 2
    return (
        value[:channels, :size] - value[channels:, size:],
        value[:channels, size:] + value[channels:, :size],
    )


def last_halo_kernel(level, halo, high, low, sums, refl_level, refl_coef, out):
    def add(b, value):
        re, im = leaving(sums[b] + value)
        lanes = slice(b * re.shape[1], (b + 1) * re.shape[1])
        re, im = reflected(
            re,
            im,
            refl_level[:, lanes] == level + 1,
            refl_coef[0:1, lanes],
            refl_coef[1:2, lanes],
        )
        out[0, :, lanes] = re
        out[1, :, lanes] = im

    add_halo(halo, high, low, lax.axis_index("lat") % 2 == 0, add)


def bottom_kernel(halo, high, low, sums, out, held, sems):
    panels, _, part, _ = out.shape
    block_rows, _, size, _ = high.shape

    def copy_out(b):
        lanes = pl.ds(b * size, size)
        return pltpu.make_async_copy(
            held.at[b], out.at[:, :, :, lanes], sems.at[b]
        )

    def add(b, value):
        re, im = leaving(sums[b] + value)
        held[b, :, 0] = re.reshape(panels, part, size)
        held[b, :, 1] = im.reshape(panels, part, size)
        copy_out(b).start()

    add_halo(halo, high, low, lax.axis_index("lat") % 2 == 0, add)
    for b in range(block_rows):
        copy_out(b).wait()


def in_hbm(value):
    return pltpu.with_memory_space_constraint(value, pltpu.HBM)


def params(mib):
    return pltpu.CompilerParams(vmem_limit_bytes=mib * MIB)


def cost(flops, transferred):
    return pl.CostEstimate(flops=flops, bytes_accessed=transferred, transcendentals=0)


def per_device(sources, blocks, block_cols, refl_level, refl_coef):
    lat_count = lax.axis_size("lat")
    panels, _, part, points = sources.shape
    _, block_rows, per_row, _, size, _ = blocks.shape
    channels = panels * part
    f32, bf16 = jnp.float32, jnp.bfloat16
    axes = ("depth", "lat")
    over_depth = [(0, 1), (1, 0)]
    even = range(0, lat_count - 1, 2)
    uneven = range(1, lat_count - 1, 2)
    alone_even = range(lat_count - lat_count % 2, lat_count)
    alone_uneven = [0] + list(range(lat_count - 1 + lat_count % 2, lat_count))

    def over_lat(firsts, alone):
        pairs = [(d * lat_count + i, d * lat_count + i + 1) for d in range(2) for i in firsts]
        pairs += [(i, lat_count + i) for i in alone]
        return pairs + [(j, i) for i, j in pairs]

    refl_level = refl_level.reshape(1, points)
    other_blocks = lax.ppermute(blocks, "depth", over_depth)
    other_cols = lax.ppermute(block_cols, "depth", over_depth)
    field_shape = jax.ShapeDtypeStruct((2, channels, points), f32)
    total = pl.pallas_call(
        enter_kernel,
        out_shape=field_shape,
        in_specs=[HBM] * 3,
        out_specs=VMEM,
        scratch_shapes=[
            pltpu.VMEM(sources.shape, f32),
            pltpu.VMEM((1, points), jnp.int32),
            pltpu.VMEM((2, points), f32),
            pltpu.SemaphoreType.DMA((3,)),
        ],
        compiler_params=params(4),
        name="enter",
    )(in_hbm(sources), in_hbm(refl_level), in_hbm(refl_coef))

    band_shape = jax.ShapeDtypeStruct((block_rows, 2 * block_rows + 1, size, 2 * size), bf16)
    sums_shape = jax.ShapeDtypeStruct((block_rows, 2 * channels, 2 * size), f32)
    macs = 6 * channels * points * 2 * size
    for level in range(2):
        diagonal = lax.ppermute(total, axes, over_lat(uneven, alone_uneven))
        swapped = lax.ppermute(total, axes, over_lat(even, alone_even))
        high, low, sums = pl.pallas_call(
            functools.partial(prepare_kernel, level),
            out_shape=[band_shape, band_shape, sums_shape],
            in_specs=[SMEM, SMEM, HBM, HBM, VMEM],
            out_specs=[VMEM] * 3,
            scratch_shapes=[
                pltpu.VMEM(blocks.shape[1:], f32),
                pltpu.SemaphoreType.DMA((block_rows,)),
            ],
            compiler_params=params(16),
            cost_estimate=cost(4 * macs, 8 * blocks.size),
            name="prepare",
        )(in_hbm(block_cols), other_cols, in_hbm(blocks), other_blocks, total)
        sums = pl.pallas_call(
            first_halo_kernel,
            out_shape=sums_shape,
            in_specs=[VMEM] * 4,
            out_specs=VMEM,
            compiler_params=params(12),
            cost_estimate=cost(macs, blocks.size),
            name="first_halo",
        )(swapped, high, low, sums)
        if level == 0:
            total = pl.pallas_call(
                functools.partial(last_halo_kernel, level),
                out_shape=field_shape,
                in_specs=[VMEM] * 6,
                out_specs=VMEM,
                compiler_params=params(12),
                cost_estimate=cost(macs, blocks.size),
                name="last_halo",
            )(diagonal, high, low, sums, refl_level, refl_coef)
    return pl.pallas_call(
        bottom_kernel,
        out_shape=jax.ShapeDtypeStruct(sources.shape, f32),
        in_specs=[VMEM] * 4,
        out_specs=HBM,
        scratch_shapes=[
            pltpu.VMEM((block_rows, panels, 2, part, size), f32),
            pltpu.SemaphoreType.DMA((block_rows,)),
        ],
        compiler_params=params(12),
        cost_estimate=cost(macs, blocks.size),
        name="bottom",
    )(diagonal, high, low, sums)


def solution(mesh):
    placed = (
        P("shot", None, "depth", "lat"),
        P(("shot", "depth"), "lat", None, None, None, None),
        P("depth", "lat", None),
        P("lat"),
        P(None, "lat"),
    )
    return jax.shard_map(
        per_device,
        mesh=mesh,
        in_specs=placed,
        out_specs=P("shot", None, "depth", "lat"),
        check_vma=False,
    )
```

time: 67.7 us -> 26.7 us (0.39)
  between operations: 13.7 us -> 0.07 us
  waiting for transfers between devices: 20.5 us -> 7.98 us
  Pallas kernels: 0 us -> 12.1 us
  local copies, waits for them, and re-layouts: 10 us -> 0.26 us
  matrix products: 8.14 us -> 0 us
  starting transfers between devices: 12.7 us -> 6.07 us
  blocking collectives: 1.84 us -> 0 us
    pallas_call x0 -> x7, Pallas kernels: none -> 12.1 us  [the longest x2 8.73 us: per_device(): pl.pallas_call(functools.partial(prepare_kernel, level), out_shape=[band_...]
    dot_general x4 -> x0, matrix products: 8.14 us -> none  [the longest x2 4.89 us: per_device(): jnp.einsum('cbjp,bjpq->bcq', picked, level_blocks[:, :, 1], precision=lax...]
    all_gather x1 -> x0, waiting for transfers between devices: 7.07 us -> none  [per_device(): lax.all_gather(blocks, 'depth', axis=0, tiled=True)]
    ppermute x4 -> x6, starting transfers between devices: 12.7 us -> 6.07 us  [the longest x2 5.07 us: per_device(): swapped = lax.ppermute(total, axes, over_lat(even, alone_even))]
    ppermute x4 -> x6, waiting for transfers between devices: 12.7 us -> 7.98 us  [the longest x2 5.49 us: per_device(): swapped = lax.ppermute(total, axes, over_lat(even, alone_even))]
    slice x6 -> x0, local copies, waits for them, and re-layouts: 4.21 us -> none  [the longest x1 4.09 us: per_device(): level_blocks = every_blocks[level_global]]
    squeeze x1 -> x0, local copies, waits for them, and re-layouts: 2.74 us -> none  [per_device(): level_blocks = every_blocks[level_global]]
    all_gather x1 -> x0, blocking collectives: 1.84 us -> none  [per_device(): lax.all_gather(block_cols, 'depth', axis=0, tiled=True)]
  transfers between devices with their start and end apart: 5 -> 6, of which waited for: 5 -> 3; matrix products, arithmetic and copies ran while one was open for 2% -> 0% of each run, Pallas kernels for 0% -> 40%
where the time goes in v2:
time: 26.7 us; the launch traced here: 26.5 us
  Pallas kernels  12.1 us (45%)
  waiting for transfers between devices  7.98 us (30%)
  starting transfers between devices  6.07 us (23%)
    pallas_call x2, Pallas kernels, per_device(): pl.pallas_call(functools.partial(prepare_kernel, level), out_shape=[band_...  8.73 us
    ppermute x2, waiting for transfers between devices, per_device(): swapped = lax.ppermute(total, axes, over_lat(even, alone_even))  5.49 us
    ppermute x2, starting transfers between devices, per_device(): swapped = lax.ppermute(total, axes, over_lat(even, alone_even))  5.07 us
    ppermute x1, waiting for transfers between devices, per_device(): other_cols = lax.ppermute(block_cols, 'depth', over_depth)  2.48 us
    pallas_call x1, Pallas kernels, per_device(): pl.pallas_call(bottom_kernel, out_shape=jax.ShapeDtypeStruct(sources.shap...  1.11 us
    pallas_call x1, Pallas kernels, per_device(): pl.pallas_call(enter_kernel, out_shape=field_shape, in_specs=[HBM] * 3, o...  0.99 us
    pallas_call x2, Pallas kernels, per_device(): pl.pallas_call(first_halo_kernel, out_shape=sums_shape, in_specs=[VMEM] *...  0.84 us
  transfers between devices with their start and end apart: 6, of which 3 were waited for; matrix products, arithmetic and copies ran while one was open for 0% of the time, Pallas kernels for 40%

profile of v2, /device:TPU:0, one launch (start us, length us, event | category | flops | bytes accessed | tf_op | source)
XLA Modules:
  0.0 26.5 jit_solution(12946663683939145566)
XLA Ops:
  0.0 0.5 %collective-permute-start.2 = (f32[1,4,7,2,128,128]{5,4,3,2,1,0:T(8,128)}, f32[1,4,7,2,128,128]{5,4,3,2,1,0:T(8,128)S(1)}, u32[]{:S(2)}, u32[]{:S(2)}) collective-permute-start(f32[1,4,7,2,128,128]{5,4,3,2,1,0:T(8,128)} %own.3), channel_id=1, source_target_pairs={{0,8},{8,0},{1,9},{9,1},{2,10},{10,2},{3,11},{11,3},{4,12},{12,4},... | collective-permute-start | bytes 11010056 | tf_op jit(solution)/shard_map/ppermute | solution.py:223
  0.5 1.0 %enter.1.field = f32[2,48,512]{2,1,0:T(8,128)S(1)} custom-call(f32[3,2,16,512]{3,2,1,0:T(8,128)} %sources.1, s32[1,512]{1,0:T(1,128)} %bitcast.1, f32[2,512]{1,0:T(2,128)} %refl_coef.3), custom_call_target="tpu_custom_call" | custom-call | tf_op jit(solution)/shard_map/enter/pallas_call | solution.py:226
  1.5 2.5 %collective-permute-start.3 = (f32[2,48,512]{2,1,0:T(8,128)S(1)}, f32[2,48,512]{2,1,0:T(8,128)S(1)}, u32[]{:S(2)}, u32[]{:S(2)}) collective-permute-start(f32[2,48,512]{2,1,0:T(8,128)S(1)} %enter.1.field), channel_id=1, source_target_pairs={{0,1},{2,3},{4,5},{6,7},{8,9},{10,11},{12,13},{14,15},{1,0},{3,2},... | collective-permute-start | bytes 589832 | tf_op jit(solution)/shard_map/ppermute | solution.py:246
  4.0 0.2 collective-permute-start
  4.3 0.3 %collective-permute-start.1 = (s32[1,4,7]{2,1,0:T(4,128)}, s32[1,4,7]{2,1,0:T(4,128)S(1)}, u32[]{:S(2)}, u32[]{:S(2)}) collective-permute-start(s32[1,4,7]{2,1,0:T(4,128)} %own_cols.3), channel_id=1, source_target_pairs={{0,8},{8,0},{1,9},{9,1},{2,10},{10,2},{3,11},{11,3},{4,12},{12,4},... | collective-permute-start | bytes 344 | tf_op jit(solution)/shard_map/ppermute | solution.py:224
  4.5 2.5 %collective-permute-done.1.other_cols = s32[1,4,7]{2,1,0:T(4,128)S(1)} collective-permute-done((s32[1,4,7]{2,1,0:T(4,128)}, s32[1,4,7]{2,1,0:T(4,128)S(1)}, u32[]{:S(2)}, u32[]{:S(2)}) %collective-permute-start.1) | collective-permute-done | bytes 144 | tf_op jit(solution)/shard_map/ppermute | solution.py:224
  7.0 0.0 collective-permute-done.2.received
  7.0 4.4 %prepare.2 = (bf16[4,9,128,256]{3,2,1,0:T(8,128)(2,1)S(1)}, bf16[4,9,128,256]{3,2,1,0:T(8,128)(2,1)S(1)}, f32[4,96,256]{2,1,0:T(8,128)S(1)}) custom-call(s32[1,4,7]{2,1,0:T(4,128)} %own_cols.3, s32[1,4,7]{2,1,0:T(4,128)S(1)} %collective-permute-done.1.other_cols, f32[1,4,7,2,128,128]{5,4,3,2,1,0:T(8,128)} %own.3, ...), custom_call_target="tpu_custom_call" | custom-call | flops 150994944 | bytes 7340032 | tf_op jit(solution)/shard_map/prepare/pallas_call | solution.py:247
  11.4 1.6 %collective-permute-done.3.halo = f32[2,48,512]{2,1,0:T(8,128)S(1)} collective-permute-done((f32[2,48,512]{2,1,0:T(8,128)S(1)}, f32[2,48,512]{2,1,0:T(8,128)S(1)}, u32[]{:S(2)}, u32[]{:S(2)}) %collective-permute-start.3) | collective-permute-done | bytes 196640 | tf_op jit(solution)/shard_map/ppermute | solution.py:246
  13.1 0.0 copy-start
  13.1 0.0 copy-start.1
  13.1 0.4 %first_halo.2.sums = f32[4,96,256]{2,1,0:T(8,128)S(1)} custom-call(f32[2,48,512]{2,1,0:T(8,128)S(1)} %collective-permute-done.3.halo, bf16[4,9,128,256]{3,2,1,0:T(8,128)(2,1)S(1)} %get-tuple-element.11.high, bf16[4,9,128,256]{3,2,1,0:T(8,128)(2,1)S(1)} %get-tuple-element.12.low, f32[4,96,256]{2,1,0:T(8,128)S(1)} %get-tuple-element.13.sums), custom_call_target="tpu_custom_call" | custom-call | flops 37748736 | bytes 917504 | tf_op jit(solution)/shard_map/first_halo/pallas_call | solution.py:260
  13.5 0.0 collective-permute-done.halo
  13.5 0.2 copy-done
  13.8 0.0 copy-done.1
  13.8 0.5 %last_halo.1.field = f32[2,48,512]{2,1,0:T(8,128)S(1)} custom-call(f32[2,48,512]{2,1,0:T(8,128)S(1)} %collective-permute-done.halo, bf16[4,9,128,256]{3,2,1,0:T(8,128)(2,1)S(1)} %get-tuple-element.11.high, bf16[4,9,128,256]{3,2,1,0:T(8,128)(2,1)S(1)} %get-tuple-element.12.low, f32[4,96,256]{2,1,0:T(8,128)S(1)} %first_halo.2.sums, s32[1,512]{1,0:T(1,128)S(1)} %bitcast.2, ...), custom_call_target="tpu_custom_call" | custom-call | flops 37748736 | bytes 917504 | tf_op jit(solution)/shard_map/last_halo/pallas_call | solution.py:270
  14.2 2.5 %collective-permute-start.5 = (f32[2,48,512]{2,1,0:T(8,128)S(1)}, f32[2,48,512]{2,1,0:T(8,128)S(1)}, u32[]{:S(2)}, u32[]{:S(2)}) collective-permute-start(f32[2,48,512]{2,1,0:T(8,128)S(1)} %last_halo.1.field), channel_id=1, source_target_pairs={{0,1},{2,3},{4,5},{6,7},{8,9},{10,11},{12,13},{14,15},{1,0},{3,2},... | collective-permute-start | bytes 589832 | tf_op jit(solution)/shard_map/ppermute | solution.py:246
  16.8 0.0 collective-permute-start.4
  16.8 4.3 %prepare.3 = (bf16[4,9,128,256]{3,2,1,0:T(8,128)(2,1)S(1)}, bf16[4,9,128,256]{3,2,1,0:T(8,128)(2,1)S(1)}, f32[4,96,256]{2,1,0:T(8,128)S(1)}) custom-call(s32[1,4,7]{2,1,0:T(4,128)} %own_cols.3, s32[1,4,7]{2,1,0:T(4,128)S(1)} %collective-permute-done.1.other_cols, f32[1,4,7,2,128,128]{5,4,3,2,1,0:T(8,128)} %own.3, ...), custom_call_target="tpu_custom_call" | custom-call | flops 150994944 | bytes 7340032 | tf_op jit(solution)/shard_map/prepare/pallas_call | solution.py:247
  21.1 3.9 %collective-permute-done.5.halo = f32[2,48,512]{2,1,0:T(8,128)S(1)} collective-permute-done((f32[2,48,512]{2,1,0:T(8,128)S(1)}, f32[2,48,512]{2,1,0:T(8,128)S(1)}, u32[]{:S(2)}, u32[]{:S(2)}) %collective-permute-start.5) | collective-permute-done | bytes 196640 | tf_op jit(solution)/shard_map/ppermute | solution.py:246
  24.9 0.4 %first_halo.3.sums = f32[4,96,256]{2,1,0:T(8,128)S(1)} custom-call(f32[2,48,512]{2,1,0:T(8,128)S(1)} %collective-permute-done.5.halo, bf16[4,9,128,256]{3,2,1,0:T(8,128)(2,1)S(1)} %get-tuple-element.14.high, bf16[4,9,128,256]{3,2,1,0:T(8,128)(2,1)S(1)} %get-tuple-element.15.low, f32[4,96,256]{2,1,0:T(8,128)S(1)} %get-tuple-element.16.sums), custom_call_target="tpu_custom_call" | custom-call | flops 37748736 | bytes 917504 | tf_op jit(solution)/shard_map/first_halo/pallas_call | solution.py:260
  25.4 0.0 collective-permute-done.4.halo
  25.4 1.1 %bottom.1 = f32[3,2,16,512]{3,2,1,0:T(8,128)} custom-call(f32[2,48,512]{2,1,0:T(8,128)S(1)} %collective-permute-done.4.halo, bf16[4,9,128,256]{3,2,1,0:T(8,128)(2,1)S(1)} %get-tuple-element.14.high, bf16[4,9,128,256]{3,2,1,0:T(8,128)(2,1)S(1)} %get-tuple-element.15.low, f32[4,96,256]{2,1,0:T(8,128)S(1)} %first_halo.3.sums), custom_call_target="tpu_custom_call" | custom-call | flops 37748736 | bytes 917504 | tf_op jit(solution)/shard_map/bottom/pallas_call | solution.py:279
Async XLA Ops:
  0.0 7.0 %collective-permute-start.2 = (f32[1,4,7,2,128,128]{5,4,3,2,1,0:T(8,128)}, f32[1,4,7,2,128,128]{5,4,3,2,1,0:T(8,128)S(1)}, u32[]{:S(2)}, u32[]{:S(2)}) collective-permute-start(f32[1,4,7,2,128,128]{5,4,3,2,1,0:T(8,128)} %own.3), channel_id=1, source_target_pairs={{0,8},{8,0},{1,9},{9,1},{2,10},{10,2},{3,11},{11,3},{4,12},{12,4},... | collective-permute-start | bytes 11010056 | tf_op jit(solution)/shard_map/ppermute | solution.py:223
  1.5 11.6 %collective-permute-start.3 = (f32[2,48,512]{2,1,0:T(8,128)S(1)}, f32[2,48,512]{2,1,0:T(8,128)S(1)}, u32[]{:S(2)}, u32[]{:S(2)}) collective-permute-start(f32[2,48,512]{2,1,0:T(8,128)S(1)} %enter.1.field), channel_id=1, source_target_pairs={{0,1},{2,3},{4,5},{6,7},{8,9},{10,11},{12,13},{14,15},{1,0},{3,2},... | collective-permute-start | bytes 589832 | tf_op jit(solution)/shard_map/ppermute | solution.py:246
  4.0 9.5 %collective-permute-start = (f32[2,48,512]{2,1,0:T(8,128)S(1)}, f32[2,48,512]{2,1,0:T(8,128)S(1)}, u32[]{:S(2)}, u32[]{:S(2)}) collective-permute-start(f32[2,48,512]{2,1,0:T(8,128)S(1)} %enter.1.field), channel_id=1, source_target_pairs={{1,2},{3,4},{5,6},{9,10},{11,12},{13,14},{0,8},{7,15},{2,1},{4,3},... | collective-permute-start | bytes 589832 | tf_op jit(solution)/shard_map/ppermute | solution.py:245
  4.3 2.8 %collective-permute-start.1 = (s32[1,4,7]{2,1,0:T(4,128)}, s32[1,4,7]{2,1,0:T(4,128)S(1)}, u32[]{:S(2)}, u32[]{:S(2)}) collective-permute-start(s32[1,4,7]{2,1,0:T(4,128)} %own_cols.3), channel_id=1, source_target_pairs={{0,8},{8,0},{1,9},{9,1},{2,10},{10,2},{3,11},{11,3},{4,12},{12,4},... | collective-permute-start | bytes 344 | tf_op jit(solution)/shard_map/ppermute | solution.py:224
  13.1 0.7 %copy-start = (f32[2,512]{1,0:T(2,128)S(1)}, f32[2,512]{1,0:T(2,128)}, u32[]{:S(2)}) copy-start(f32[2,512]{1,0:T(2,128)} %refl_coef.3) | copy-start | bytes 12292
  13.1 0.7 %copy-start.1 = (s32[512]{0:T(512)S(1)}, s32[512]{0:T(512)}, u32[]{:S(2)}) copy-start(s32[512]{0:T(512)} %param.8) | copy-start | bytes 6148
  14.2 10.7 %collective-permute-start.5 = (f32[2,48,512]{2,1,0:T(8,128)S(1)}, f32[2,48,512]{2,1,0:T(8,128)S(1)}, u32[]{:S(2)}, u32[]{:S(2)}) collective-permute-start(f32[2,48,512]{2,1,0:T(8,128)S(1)} %last_halo.1.field), channel_id=1, source_target_pairs={{0,1},{2,3},{4,5},{6,7},{8,9},{10,11},{12,13},{14,15},{1,0},{3,2},... | collective-permute-start | bytes 589832 | tf_op jit(solution)/shard_map/ppermute | solution.py:246
  16.8 8.6 %collective-permute-start.4 = (f32[2,48,512]{2,1,0:T(8,128)S(1)}, f32[2,48,512]{2,1,0:T(8,128)S(1)}, u32[]{:S(2)}, u32[]{:S(2)}) collective-permute-start(f32[2,48,512]{2,1,0:T(8,128)S(1)} %last_halo.1.field), channel_id=1, source_target_pairs={{1,2},{3,4},{5,6},{9,10},{11,12},{13,14},{0,8},{7,15},{2,1},{4,3},... | collective-permute-start | bytes 589832 | tf_op jit(solution)/shard_map/ppermute | solution.py:245
